TPU v7x, 32 devices: a whole 2x2x4 slice. The times are simulated.
32 devices in a mesh: grp: 2 (over x), row: 8 (over z, y), col: 2 (over core).
Axes of the slice: x: 2, y: 2, z: 4, core: 2. Of those that a mesh axis runs over, the one named last changes fastest.
Arguments:
- queries: bfloat16 [128, 32, 1024], P(('grp', 'row'), 'col'), parts along dimension 0, may hold values from -4 to 4
- key_map: bfloat16 [128, 32, 1024], P(('grp', 'row'), 'col'), parts along dimension 0, may hold values from -4 to 4
- value_map: bfloat16 [128, 32, 1024], P(('grp', 'row'), 'col'), parts along dimension 0, may hold values from -4 to 4
- saved_output: bfloat16 [128, 32, 1024], P(('grp', 'row'), 'col'), parts along dimension 0, may hold values from -4 to 4, as said below
- output_grad: bfloat16 [128, 32, 1024], P(('grp', 'row'), 'col'), parts along dimension 0, may hold values from -48 to 48
- saved_logsum: float32 [128, 32, 16], P(('grp', 'row'), 'col'), parts along dimension 0, may hold values from -128 to 140, as said below
Outputs:
- query_grad: float32 [128, 32, 1024], P(('grp', 'row'), 'col'), parts along dimension 0
- key_grad: float32 [128, 32, 1024], P(('grp', 'row'), 'col'), parts along dimension 0
- value_grad: float32 [128, 32, 1024], P(('grp', 'row'), 'col'), parts along dimension 0
There are 2 independent parts, one for each index of `grp`. A program takes and returns all parts, laid end to end along the dimension named above; each array names one. Nothing has to cross between parts.
Inputs may be any that keep to these rules, and one draw needn't show every extreme that they name: `saved_output`: the attention output of these queries, keys and values over the stripes of the steps, sum over j of softmax of scores times value_map[j], rounded to bfloat16. `saved_logsum`: for each token and head, the natural logarithm of the sum of exp(scores) over the keys of its stripe.
All inputs are finite; a program needn't handle non-finite values.
Results may differ from a plain program's by a relative error of at most 0.003.
Values may be sent and summed in bfloat16 or wider, within the bound.
A program may use at most 128 MiB of HBM per device.

v0:
```python
import math

import jax
import jax.numpy as jnp
from jax import lax
from jax.sharding import PartitionSpec as P

HEADS = 16
HD = 64
SW = 8


def attention_terms(
    stripe_query, stripe_key, stripe_value, stripe_grad, stripe_logsum, stripe_delta
):
    scale = 1.0 / math.sqrt(HD)
    scores = (
        jnp.einsum("gahe,gbhe->ghab", stripe_query, stripe_key, preferred_element_type=jnp.float32)
        * scale
    )
    probs = jnp.exp(scores - jnp.swapaxes(stripe_logsum, 1, 2)[..., None])
    grad_probs = jnp.einsum(
        "gahe,gbhe->ghab", stripe_grad, stripe_value, preferred_element_type=jnp.float32
    )
    grad_scores = (probs * (grad_probs - jnp.swapaxes(stripe_delta, 1, 2)[..., None])).astype(
        jnp.bfloat16
    )
    return (probs.astype(jnp.bfloat16), grad_scores)


def query_side(grad_scores, stripe_key):
    total = jnp.einsum(
        "ghab,gbhe->gahe", grad_scores, stripe_key, preferred_element_type=jnp.float32
    )
    return total * (1.0 / math.sqrt(HD))


def key_side(probs_half, grad_scores, stripe_query, stripe_grad):
    key_total = jnp.einsum(
        "ghab,gahe->gbhe", grad_scores, stripe_query, preferred_element_type=jnp.float32
    )
    value_total = jnp.einsum(
        "ghab,gahe->gbhe", probs_half, stripe_grad, preferred_element_type=jnp.float32
    )
    return (key_total * (1.0 / math.sqrt(HD)), value_total)


def in_blocks(step, carry, arrays, size):
    length = arrays[0].shape[0]

    def turn(index, total):
        parts = tuple((lax.dynamic_slice_in_dim(array, index * size, size, 0) for array in arrays))
        return step(total, parts)

    return lax.fori_loop(0, length // size, turn, carry)


def local(queries, key_map, value_map, saved_output, output_grad, saved_logsum):
    rows, cols, width = queries.shape
    half = HEADS // 2
    split = half * HD
    tail = (half, HD)
    block = 4 * rows
    products = output_grad.astype(jnp.float32) * saved_output.astype(jnp.float32)
    delta_all = jnp.sum(products.reshape(rows, cols, HEADS, HD), axis=3)

    def row_group(values, last):
        return values.reshape((rows // SW, SW * values.shape[1]) + last)

    def column_group(values, last):
        count = values.shape[0]
        shaped = values.reshape((count, cols // SW, SW) + last)
        return jnp.swapaxes(shaped, 0, 1).reshape((cols // SW, count * SW) + last)

    def column_back(values, count):
        shaped = values.reshape((cols // SW, count, SW, -1))
        return jnp.swapaxes(shaped, 0, 1).reshape(count, cols, -1)

    full_key, full_value = (
        lax.all_gather(key_map[:, :, :split], "col", axis=1, tiled=True),
        lax.all_gather(value_map[:, :, :split], "col", axis=1, tiled=True),
    )
    wide = full_key.shape[1]
    stripe_query = row_group(queries[:, :, :split], tail)
    stripe_grad = row_group(output_grad[:, :, :split], tail)
    stripe_logsum = row_group(saved_logsum[:, :, :half], (half,))
    stripe_delta = row_group(delta_all[:, :, :half], (half,))
    stripe_key = row_group(full_key, tail)
    stripe_value = row_group(full_value, tail)
    probs_half, grad_scores = attention_terms(
        stripe_query, stripe_key, stripe_value, stripe_grad, stripe_logsum, stripe_delta
    )
    row_query_grad = query_side(grad_scores, stripe_key).reshape(rows, cols, split)
    row_key_part, row_value_part = key_side(probs_half, grad_scores, stripe_query, stripe_grad)
    row_term = jnp.concatenate(
        (row_key_part.reshape(rows, wide, split), row_value_part.reshape(rows, wide, split)), axis=2
    )
    row_sums = lax.psum_scatter(row_term, "col", scatter_dimension=1, tiled=True)
    local_key = key_map[:, :, split:]
    local_value = value_map[:, :, split:]
    column_query = column_group(queries[:, :, split:], tail)
    column_grad = column_group(output_grad[:, :, split:], tail)
    column_logsum = column_group(saved_logsum[:, :, half:], (half,))
    column_delta = column_group(delta_all[:, :, half:], (half,))

    def query_step(total, pieces):
        grouped_key = column_group(pieces[0], tail)
        grouped_value = column_group(pieces[1], tail)
        weights, gradients = attention_terms(
            column_query, grouped_key, grouped_value, column_grad, column_logsum, column_delta
        )
        return total + query_side(gradients, grouped_key)

    empty_query = jnp.zeros(column_query.shape, jnp.float32)
    every_key, every_value = (
        lax.all_gather(local_key, "row", axis=0, tiled=True),
        lax.all_gather(local_value, "row", axis=0, tiled=True),
    )
    column_total = in_blocks(query_step, empty_query, (every_key, every_value), block)

    def key_step(pieces):
        count = pieces[0].shape[0]
        grouped_key = column_group(pieces[0], tail)
        grouped_value = column_group(pieces[1], tail)
        weights, gradients = attention_terms(
            column_query, grouped_key, grouped_value, column_grad, column_logsum, column_delta
        )
        key_part, value_part = key_side(weights, gradients, column_query, column_grad)
        return jnp.concatenate(
            (column_back(key_part, count), column_back(value_part, count)), axis=2
        )

    count = rows * lax.axis_size("row")
    stacked = lax.map(
        key_step,
        (
            every_key.reshape((count // block, block) + every_key.shape[1:]),
            every_value.reshape((count // block, block) + every_value.shape[1:]),
        ),
    )
    column_sums = lax.psum_scatter(
        stacked.reshape((count,) + stacked.shape[2:]), "row", scatter_dimension=0, tiled=True
    )
    column_key_grad = column_sums[:, :, :split]
    column_value_grad = column_sums[:, :, split:]
    column_query_grad = column_back(column_total, rows)
    query_grad = jnp.concatenate((row_query_grad, column_query_grad), axis=2)
    key_grad = jnp.concatenate((row_sums[:, :, :split], column_key_grad), axis=2)
    value_grad = jnp.concatenate((row_sums[:, :, split:], column_value_grad), axis=2)
    return (query_grad, key_grad, value_grad)


def solution(mesh):
    in_specs = (
        P(("grp", "row"), "col", None),
        P(("grp", "row"), "col", None),
        P(("grp", "row"), "col", None),
        P(("grp", "row"), "col", None),
        P(("grp", "row"), "col", None),
        P(("grp", "row"), "col", None),
    )
    out_specs = (
        P(("grp", "row"), "col", None),
        P(("grp", "row"), "col", None),
        P(("grp", "row"), "col", None),
    )
    return jax.shard_map(local, mesh=mesh, in_specs=in_specs, out_specs=out_specs, check_vma=False)
```

profile of v0, /device:TPU:0, one launch (start us, length us, event | category | flops | bytes accessed | tf_op | source)
XLA Modules:
  0.0 230.9 jit_solution(451609579921056078)
XLA Ops:
  8.1 1.7 fusion.35
  9.8 1.6 fusion.33
  11.5 1.0 fusion.36
  12.5 1.0 fusion.38
  14.0 2.1 all_gather.12
  16.7 2.0 all_gather.13
  21.1 0.8 copy-done.6
  23.7 1.1 pad_maximum_fusion
  26.3 28.2 %all-gather.3.cloned.1.call-done = bf16[64,16,512]{2,1,0:T(8,128)(2,1)} async-done(((bf16[8,16,512]{2,1,0:T(8,128)(2,1)}), bf16[64,16,512]{2,1,0:T(8,128)(2,1)}) %all-gather.3.cloned.1.call-update) | async-done | bytes 1048592 | tf_op jit(solution)/shard_map/all_gather | solution.py:116
  54.5 41.1 %all-gather.5.cloned.1.call-done = bf16[64,16,512]{2,1,0:T(8,128)(2,1)} async-done(((bf16[8,16,512]{2,1,0:T(8,128)(2,1)}), bf16[64,16,512]{2,1,0:T(8,128)(2,1)}) %all-gather.5.cloned.1.call-update) | async-done | bytes 1048592 | tf_op jit(solution)/shard_map/all_gather | solution.py:117
  95.6 38.5 %while.24 = (s32[]{:T(128)}, f32[2,32,16,1024]{3,2,1,0:T(8,128)}, bf16[2,32,16,512]{3,2,1,0:T(8,128)(2,1)}, bf16[2,64,8,64]{1,3,2,0:T(8,128)(2,1)S(1)}, f32[2,64...) while((s32[]{:T(128)}, f32[2,32,16,1024]{3,2,1,0:T(8,128)}, ...), condition=%wide.region_5.6_spmd, body=%wide.region_4.5_spmd.sunk | while | flops 136577024 | bytes 35135680 | solution.py:134
  95.6 2.2 constant_dynamic-slice_fusion.6
  98.9 1.4 convolution_bitcast_fusion.3
  100.3 2.0 copy.157
  102.3 1.6 reshape.209
  103.8 2.4 %copy_bitcast_fusion.7 = f32[32,16,512]{2,1,0:T(8,128)} fusion(f32[2,32,8,512]{3,2,1,0:T(8,128)} %reshape.209), kind=kLoop, calls=%fused_computation.11.clone.1 | loop fusion | bytes 2097152 | tf_op jit(solution)/shard_map/while/body/eval_jaxpr/reshape | solution.py:77
  106.2 1.6 reshape.210
  108.0 1.6 fusion.86
  109.6 0.8 copy.159
  110.4 1.6 reshape.211
  112.0 1.3 copy_bitcast_fusion.8
  113.3 1.5 fusion.87
  114.8 2.2 constant_dynamic-slice_fusion.6
  118.1 1.4 convolution_bitcast_fusion.3
  119.5 2.0 copy.157
  121.5 1.6 reshape.209
  123.1 2.4 %copy_bitcast_fusion.7 = f32[32,16,512]{2,1,0:T(8,128)} fusion(f32[2,32,8,512]{3,2,1,0:T(8,128)} %reshape.209), kind=kLoop, calls=%fused_computation.11.clone.1 | loop fusion | bytes 2097152 | tf_op jit(solution)/shard_map/while/body/eval_jaxpr/reshape | solution.py:77
  125.5 1.6 reshape.210
  127.2 1.6 fusion.86
  128.9 0.8 copy.159
  129.7 1.6 reshape.211
  131.2 1.3 copy_bitcast_fusion.8
  132.6 1.5 fusion.87
  134.1 1.0 copy-done.7
  135.7 0.9 reshape.182
  136.6 10.4 %while.25 = (s32[]{:T(128)}, f32[2,64,8,64]{1,3,2,0:T(8,128)S(1)}, bf16[64,16,512]{2,1,0:T(8,128)(2,1)}, bf16[2,64,8,64]{3,1,2,0:T(8,128)(2,1)}, f32[2,64,8]{1,2...) while((s32[]{:T(128)}, f32[2,64,8,64]{1,3,2,0:T(8,128)S(1)}, ...), condition=%wide.region_2.0_spmd.clone, body=%wide.region_1.0_spmd.clone.sunk | while | flops 102170624 | bytes 11280569 | solution.py:55
  136.6 1.3 constant_dynamic-slice_fusion.7
  138.5 0.6 copy.162
  140.2 1.6 fusion.93
  141.8 1.3 constant_dynamic-slice_fusion.7
  143.7 0.6 copy.162
  145.4 1.6 fusion.93
  147.4 1.8 pad_maximum_fusion.1
  149.2 1.1 fusion.31
  150.2 70.5 %reduce-scatter.5.cloned.1.call-done = f32[8,16,1024]{2,1,0:T(8,128)} async-done(((f32[64,16,1024]{2,1,0:T(8,128)}), f32[8,16,1024]{2,1,0:T(8,128)}) %reduce-scatter.5.cloned.1.call-update) | async-done | bytes 524304 | tf_op jit(solution)/shard_map/reduce_scatter | solution.py:141
  220.7 1.1 fusion.32
  221.8 0.8 pad_maximum_fusion.3
  222.6 0.8 pad_maximum_fusion.2
  (94 shorter events, 13.6 us)
Async XLA Ops:
  8.0 11.0 %copy-start.10 = (bf16[8,16,1024]{2,1,0:T(8,128)(2,1)S(1)}, bf16[8,16,1024]{2,1,0:T(8,128)(2,1)}, u32[]{:S(2)}) copy-start(bf16[8,16,1024]{2,1,0:T(8,128)(2,1)} %param.14) | copy-start | bytes 786436
  8.0 11.4 %copy-start.11 = (bf16[8,16,1024]{2,1,0:T(8,128)(2,1)S(1)}, bf16[8,16,1024]{2,1,0:T(8,128)(2,1)}, u32[]{:S(2)}) copy-start(bf16[8,16,1024]{2,1,0:T(8,128)(2,1)} %param.13) | copy-start | bytes 786436
  8.0 46.5 %all-gather.3.cloned.1.call-start = ((), (), s32[]{:S(2)}) async-start(), calls=%async_computation.2 | async-start | bytes 1179648 | tf_op jit(solution)/shard_map/all_gather | solution.py:116
  9.8 85.8 %all-gather.5.cloned.1.call-start = ((), (), s32[]{:S(2)}) async-start(), calls=%async_computation.3 | async-start | bytes 1179648 | tf_op jit(solution)/shard_map/all_gather | solution.py:117
  11.5 137.7 %reduce-scatter.3.cloned.1.call-start = ((), (), s32[]{:S(2)}) async-start(), calls=%async_computation.4 | async-start | bytes 1572864 | tf_op jit(solution)/shard_map/reduce_scatter | solution.py:98
  16.7 4.3 %copy-start.8 = (bf16[256,8,64]{0,2,1:T(8,128)(2,1)}, bf16[256,8,64]{0,2,1:T(8,128)(2,1)S(1)}, u32[]{:S(2)}) copy-start(bf16[256,8,64]{0,2,1:T(8,128)(2,1)S(1)} %copy.102) | copy-start | bytes 786436
  21.0 0.8 copy-start.6
  24.8 196.0 %reduce-scatter.5.cloned.1.call-start = ((), (), s32[]{:S(2)}) async-start(), calls=%async_computation.5 | async-start | bytes 4718592 | tf_op jit(solution)/shard_map/reduce_scatter | solution.py:141
  25.7 69.9 %copy-start.3 = (bf16[2,64,8,64]{3,1,2,0:T(8,128)(2,1)}, bf16[2,64,8,64]{3,1,2,0:T(8,128)(2,1)S(1)}, u32[]{:S(2)}) copy-start(bf16[2,64,8,64]{3,1,2,0:T(8,128)(2,1)S(1)} %get-tuple-element.411) | copy-start | bytes 393220
  25.7 69.9 %copy-start.5 = (bf16[2,64,8,64]{3,1,2,0:T(8,128)(2,1)}, bf16[2,64,8,64]{3,1,2,0:T(8,128)(2,1)S(1)}, u32[]{:S(2)}) copy-start(bf16[2,64,8,64]{3,1,2,0:T(8,128)(2,1)S(1)} %get-tuple-element.408) | copy-start | bytes 393220
  95.6 3.3 %copy-start.1 = (bf16[2,64,8,64]{1,3,2,0:T(8,128)(2,1)}, bf16[2,64,8,64]{1,3,2,0:T(8,128)(2,1)S(1)}, u32[]{:S(2)}) copy-start(bf16[2,64,8,64]{1,3,2,0:T(8,128)(2,1)S(1)} %get-tuple-element.462) | copy-start | bytes 393220 | tf_op jit(solution)/shard_map/while
  110.4 2.9 %copy-start = (f32[32,16,512]{2,1,0:T(8,128)S(1)}, f32[32,16,512]{2,1,0:T(8,128)}, u32[]{:S(2)}) copy-start(f32[32,16,512]{2,1,0:T(8,128)} %copy_bitcast_fusion.7) | copy-start | bytes 3145732 | tf_op jit(solution)/shard_map/while
  112.0 2.9 %copy-start.2 = (bf16[2,64,8,64]{1,3,2,0:T(8,128)(2,1)S(1)}, bf16[2,64,8,64]{1,3,2,0:T(8,128)(2,1)}, u32[]{:S(2)}) copy-start(bf16[2,64,8,64]{1,3,2,0:T(8,128)(2,1)} %copy-done.1) | copy-start | bytes 393220 | tf_op jit(solution)/shard_map/while
  114.8 3.3 %copy-start.1 = (bf16[2,64,8,64]{1,3,2,0:T(8,128)(2,1)}, bf16[2,64,8,64]{1,3,2,0:T(8,128)(2,1)S(1)}, u32[]{:S(2)}) copy-start(bf16[2,64,8,64]{1,3,2,0:T(8,128)(2,1)S(1)} %get-tuple-element.462) | copy-start | bytes 393220 | tf_op jit(solution)/shard_map/while
  129.6 2.9 %copy-start = (f32[32,16,512]{2,1,0:T(8,128)S(1)}, f32[32,16,512]{2,1,0:T(8,128)}, u32[]{:S(2)}) copy-start(f32[32,16,512]{2,1,0:T(8,128)} %copy_bitcast_fusion.7) | copy-start | bytes 3145732 | tf_op jit(solution)/shard_map/while
  131.2 2.8 %copy-start.2 = (bf16[2,64,8,64]{1,3,2,0:T(8,128)(2,1)S(1)}, bf16[2,64,8,64]{1,3,2,0:T(8,128)(2,1)}, u32[]{:S(2)}) copy-start(bf16[2,64,8,64]{1,3,2,0:T(8,128)(2,1)} %copy-done.1) | copy-start | bytes 393220 | tf_op jit(solution)/shard_map/while
  134.0 1.0 copy-start.7
  134.0 1.1 copy-start.9
  134.0 2.5 %copy-start.4 = (bf16[2,64,8,64]{3,1,2,0:T(8,128)(2,1)S(1)}, bf16[2,64,8,64]{3,1,2,0:T(8,128)(2,1)}, u32[]{:S(2)}) copy-start(bf16[2,64,8,64]{3,1,2,0:T(8,128)(2,1)} %copy-done.3) | copy-start | bytes 393220
Sparse Core Ops, SparseCore 0:
  11.6 42.9 all-gather.2
  56.6 38.8 all-gather.4
Sparse Core Ops, SparseCore 1:
  24.8 11.1 reduce-scatter.2
  134.2 86.5 reduce-scatter.4
where the time goes:
time: 232 us; the launch traced here: 231 us
  waiting for transfers between devices  140 us (60%)
  local copies, waits for them, and re-layouts  49.9 us (22%)
  between operations  15.8 us (7%)
  matrix products  12.7 us (5%)
  other arithmetic  7.9 us (3%)
  blocking collectives  4.08 us (2%)
    reduce_scatter x1, waiting for transfers between devices, local(): lax.psum_scatter(stacked.reshape((count,) + stacked.shape[2:]), 'row', sc...  70.5 us
    all_gather x1, waiting for transfers between devices, local(): lax.all_gather(local_value, 'row', axis=0, tiled=True)  41.1 us
    all_gather x1, waiting for transfers between devices, local(): lax.all_gather(local_key, 'row', axis=0, tiled=True)  28.2 us
    reshape x5, local copies, waits for them, and re-layouts, column_back(): return jnp.swapaxes(shaped, 0, 1).reshape(count, cols, -1)  7.5 us
    reshape x12, local copies, waits for them, and re-layouts, column_group(): shaped = values.reshape((count, cols // SW, SW) + last)  7.02 us
    reshape x5, local copies, waits for them, and re-layouts, column_back(): shaped = values.reshape((cols // SW, count, SW, -1))  6.37 us
  transfers between devices with their start and end apart: 4, of which 3 were waited for; matrix products, arithmetic and copies ran while one was open for 28% of the time, Pallas kernels for 0%

commit v1 on v0

--- a/solution.py
+++ b/solution.py
@@ -1,8 +1,11 @@
+import functools
 import math
 
 import jax
 import jax.numpy as jnp
 from jax import lax
+from jax.experimental import pallas as pl
+from jax.experimental.pallas import tpu as pltpu
 from jax.sharding import PartitionSpec as P
 
 HEADS = 16
@@ -55,7 +58,7 @@
     return lax.fori_loop(0, length // size, turn, carry)
 
 
-def local(queries, key_map, value_map, saved_output, output_grad, saved_logsum):
+def local_general(queries, key_map, value_map, saved_output, output_grad, saved_logsum):
     rows, cols, width = queries.shape
     half = HEADS // 2
     split = half * HD
@@ -150,6 +153,301 @@
     return (query_grad, key_grad, value_grad)
 
 
+MESH = pl.DeviceIdType.MESH
+NT = (((1,), (1,)), ((), ()))
+TN = (((0,), (0,)), ((), ()))
+PAIR = 2 * HD
+
+
+def flat(values):
+    return values.astype(jnp.float32).reshape((-1, values.shape[-1]))
+
+
+def attend(count, block, q_s, k_s, v_s, g_s, rows, dq_t, dk_s, dv_s):
+    scale = 1.0 / math.sqrt(HD)
+    lane = lax.broadcasted_iota(jnp.int32, (block, PAIR), 1)
+    masks = tuple(((lane // HD) == h).astype(jnp.float32).astype(jnp.bfloat16) for h in (0, 1))
+
+    def step(j, carry):
+        part = pl.ds(pl.multiple_of(j * block, block), block)
+        q = q_s[0:count, :]
+        g = g_s[0:count, :]
+        keys = k_s[part, :]
+        values = v_s[part, :]
+        dk = []
+        dv = []
+        dq = None
+        for h in (0, 1):
+            key = keys * masks[h]
+            value = values * masks[h]
+            scores = lax.dot_general(key, q, NT, preferred_element_type=jnp.float32)
+            probs = jnp.exp(scores * scale - rows[h : h + 1, 0:count])
+            grad_probs = lax.dot_general(value, g, NT, preferred_element_type=jnp.float32)
+            grad_scores = (probs * (grad_probs - rows[2 + h : 3 + h, 0:count])).astype(jnp.bfloat16)
+            half = probs.astype(jnp.bfloat16)
+            dv.append(jnp.dot(half, g, preferred_element_type=jnp.float32))
+            dk.append(jnp.dot(grad_scores, q, preferred_element_type=jnp.float32))
+            term = lax.dot_general(key, grad_scores, TN, preferred_element_type=jnp.float32)
+            dq = term if dq is None else dq + term
+        dk_s[part, :] = jnp.where(lane < HD, dk[0], dk[1]) * scale
+        dv_s[part, :] = jnp.where(lane < HD, dv[0], dv[1])
+        dq_t[:, 0:count] += dq
+        return carry
+
+    dq_t[:, 0:count] = jnp.zeros((PAIR, count), jnp.float32)
+    lax.fori_loop(0, count // block, step, 0)
+    return dq_t[:, 0:count].T * scale
+
+
+def exchange_kernel(
+    q_ref, k_ref, v_ref, o_ref, g_ref, l_ref,
+    dq_ref, dk_ref, dv_ref,
+    col_in, col_aux, row_in, row_aux, aux_row, aux_col, col_out, row_out,
+    q_s, k_s, v_s, g_s, rows_s, dq_t, dk_s, dv_s,
+    cs_sem, cr_sem, as_sem, ar_sem, rs_sem, rr_sem, os_sem, or_sem, ps_sem, pr_sem,
+):
+    me = lax.axis_index("row")
+    core = lax.axis_index("col")
+    peers = lax.axis_size("row")
+    other = 1 - core
+    split = (HEADS // 2) * HD
+    pair = me // 2
+    stripe = me % 2
+    ins = (q_ref, k_ref, v_ref, g_ref)
+    outs = (dq_ref, dk_ref, dv_ref)
+
+    barrier = pltpu.get_barrier_semaphore()
+    for step in range(1, peers):
+        pl.semaphore_signal(
+            barrier, inc=1, device_id={"row": lax.rem(me + step, peers)}, device_id_type=MESH
+        )
+    pl.semaphore_signal(barrier, inc=1, device_id={"col": other}, device_id_type=MESH)
+    pl.semaphore_wait(barrier, peers)
+
+    def col_lanes(index):
+        return pl.ds(pl.multiple_of(split + PAIR * index, PAIR), PAIR)
+
+    def core_lanes(index):
+        return pl.ds(pl.multiple_of(2 * PAIR * index, 2 * PAIR), 2 * PAIR)
+
+    def eight(index):
+        return pl.ds(pl.multiple_of(index * 8, 8), 8)
+
+    def row_copy(a):
+        return pltpu.make_async_remote_copy(
+            src_ref=ins[a].at[:, :, :, core_lanes(other)],
+            dst_ref=row_in.at[a],
+            send_sem=rs_sem.at[a], recv_sem=rr_sem.at[a],
+            device_id={"col": other}, device_id_type=MESH,
+        )
+
+    def col_copy(a, target, source):
+        return pltpu.make_async_remote_copy(
+            src_ref=ins[a].at[:, target % 2, :, col_lanes(target // 2)],
+            dst_ref=col_in.at[a, eight(source)],
+            send_sem=cs_sem.at[a, target], recv_sem=cr_sem.at[a, source],
+            device_id={"row": target}, device_id_type=MESH,
+        )
+
+    def aux_copy(target, source):
+        return pltpu.make_async_remote_copy(
+            src_ref=aux_col.at[target // 2],
+            dst_ref=col_aux.at[source],
+            send_sem=as_sem.at[target], recv_sem=ar_sem.at[source],
+            device_id={"row": target}, device_id_type=MESH,
+        )
+
+    def back_copy(a, target, owner):
+        return pltpu.make_async_remote_copy(
+            src_ref=col_out.at[a, eight(target)],
+            dst_ref=outs[a].at[:, owner % 2, :, col_lanes(owner // 2)],
+            send_sem=os_sem.at[a, target], recv_sem=or_sem.at[a, owner],
+            device_id={"row": target}, device_id_type=MESH,
+        )
+
+    def row_back(a, owner):
+        return pltpu.make_async_remote_copy(
+            src_ref=row_out.at[a],
+            dst_ref=outs[a].at[:, :, :, core_lanes(owner)],
+            send_sem=ps_sem.at[a], recv_sem=pr_sem.at[a],
+            device_id={"col": other}, device_id_type=MESH,
+        )
+
+    def row_aux_copy():
+        return pltpu.make_async_remote_copy(
+            src_ref=aux_row.at[pl.ds(2 * other, 2)],
+            dst_ref=row_aux,
+            send_sem=rs_sem.at[4], recv_sem=rr_sem.at[4],
+            device_id={"col": other}, device_id_type=MESH,
+        )
+
+    for a in range(4):
+        row_copy(a).start()
+
+    def send(step, carry):
+        target = lax.rem(me + step, peers)
+        for a in range(4):
+            col_copy(a, target, me).start()
+        return carry
+
+    lax.fori_loop(1, peers, send, 0)
+
+    which = lax.broadcasted_iota(jnp.int32, (8, PAIR), 0)
+    lane = lax.broadcasted_iota(jnp.int32, (8, PAIR), 1)
+    pick = (which == 2 + lane // HD).astype(jnp.float32)
+    which_l = lax.broadcasted_iota(jnp.int32, (8, HEADS), 0)
+    lane_l = lax.broadcasted_iota(jnp.int32, (8, HEADS), 1)
+    sums_row = flat(l_ref[...])
+    sums_col = jnp.concatenate((flat(l_ref[:, 0]), flat(l_ref[:, 1])), axis=0)
+    exact = functools.partial(
+        lax.dot_general, dimension_numbers=NT, precision=lax.Precision.HIGHEST,
+        preferred_element_type=jnp.float32,
+    )
+    for t in range(HEADS // 2):
+        part = slice(t * PAIR, (t + 1) * PAIR)
+        choose = ((lane_l - 2 * t == which_l) & (which_l < 2)).astype(jnp.float32)
+        if t < HEADS // 4:
+            products = flat(g_ref[:, :, :, part]) * flat(o_ref[:, :, :, part])
+            aux_row[t] = exact(pick, products) + exact(choose, sums_row)
+        else:
+            products = jnp.concatenate(
+                tuple(flat(g_ref[:, s, :, part]) * flat(o_ref[:, s, :, part]) for s in (0, 1)),
+                axis=0,
+            )
+            aux_col[t - HEADS // 4] = exact(pick, products) + exact(choose, sums_col)
+
+    row_aux_copy().start()
+
+    def send_aux(step, carry):
+        aux_copy(lax.rem(me + step, peers), me).start()
+        return carry
+
+    lax.fori_loop(1, peers, send_aux, 0)
+    for a in range(4):
+        col_in[a, eight(me)] = ins[a][:, stripe, :, col_lanes(pair)]
+    col_aux[me] = aux_col[pair]
+
+    for a in range(4):
+        row_copy(a).wait_recv()
+    row_aux_copy().wait_recv()
+    scratch = (q_s, k_s, v_s, g_s)
+    for u in (0, 1):
+        part = slice(u * PAIR, (u + 1) * PAIR)
+        mine = pl.ds(pl.multiple_of(2 * PAIR * core + u * PAIR, PAIR), PAIR)
+        for a in range(4):
+            scratch[a][0:128, :] = flat(ins[a][:, :, :, mine]).astype(jnp.bfloat16)
+            scratch[a][128:256, :] = flat(row_in[a, :, :, :, part]).astype(jnp.bfloat16)
+        rows_s[:, 0:128] = aux_row[2 * core + u]
+        rows_s[:, 128:256] = row_aux[u]
+        dq = attend(256, 256, q_s, k_s, v_s, g_s, rows_s, dq_t, dk_s, dv_s)
+        for a, grads in enumerate((dq, dk_s[0:256, :], dv_s[0:256, :])):
+            shaped = grads.reshape((2, 8, 2, 8, PAIR)).astype(jnp.bfloat16)
+            outs[a][:, :, :, mine] = shaped[0]
+            row_out[a, :, :, :, part] = shaped[1]
+    for a in range(3):
+        row_back(a, core).start()
+
+    def arrive(step, carry):
+        source = lax.rem(me + step, peers)
+        for a in range(4):
+            col_copy(a, source, source).wait_recv()
+        aux_copy(source, source).wait_recv()
+        return carry
+
+    lax.fori_loop(1, peers, arrive, 0)
+    for a in range(4):
+        scratch[a][...] = flat(col_in[a]).astype(jnp.bfloat16)
+    low = lane < HD
+    for k in range(4):
+        first = col_aux[2 * k]
+        second = col_aux[2 * k + 1]
+        even = jnp.where(low, first, pltpu.roll(second, HD, 1))
+        odd = jnp.where(low, pltpu.roll(first, HD, 1), second)
+        rows_s[:, k * PAIR : (k + 1) * PAIR] = jnp.where(stripe == 0, even, odd)
+    dq = attend(512, 256, q_s, k_s, v_s, g_s, rows_s, dq_t, dk_s, dv_s)
+    for a, grads in enumerate((dq, dk_s[...], dv_s[...])):
+        col_out[a] = grads.reshape((64, 8, PAIR)).astype(jnp.bfloat16)
+
+    def give(step, carry):
+        target = lax.rem(me + step, peers)
+        for a in range(3):
+            back_copy(a, target, me).start()
+        return carry
+
+    lax.fori_loop(1, peers, give, 0)
+    for a in range(3):
+        outs[a][:, stripe, :, col_lanes(pair)] = col_out[a, eight(me)]
+
+    def finish(step, carry):
+        target = lax.rem(me + step, peers)
+        for a in range(3):
+            back_copy(a, target, target).wait_recv()
+        for a in range(3):
+            back_copy(a, target, me).wait_send()
+        for a in range(4):
+            col_copy(a, target, me).wait_send()
+        aux_copy(target, me).wait_send()
+        return carry
+
+    for a in range(4):
+        row_copy(a).wait_send()
+    row_aux_copy().wait_send()
+    for a in range(3):
+        row_back(a, core).wait()
+    lax.fori_loop(1, peers, finish, 0)
+
+
+def local_exchange(peers, queries, key_map, value_map, saved_output, output_grad, saved_logsum):
+    rows, cols, width = queries.shape
+
+    def view(values):
+        return values.reshape((rows, cols // SW, SW, values.shape[-1]))
+
+    half = jnp.bfloat16
+    vmem = pl.BlockSpec(memory_space=pltpu.VMEM)
+    dma = pltpu.SemaphoreType.DMA
+    grads = pl.pallas_call(
+        exchange_kernel,
+        out_shape=(jax.ShapeDtypeStruct((rows, cols // SW, SW, width), half),) * 3,
+        in_specs=[vmem] * 6,
+        out_specs=(vmem,) * 3,
+        scratch_shapes=[
+            pltpu.VMEM((4, 8 * peers, SW, PAIR), half),
+            pltpu.VMEM((peers, 8, PAIR), jnp.float32),
+            pltpu.VMEM((4, rows, cols // SW, SW, 2 * PAIR), half),
+            pltpu.VMEM((2, 8, PAIR), jnp.float32),
+            pltpu.VMEM((4, 8, PAIR), jnp.float32),
+            pltpu.VMEM((4, 8, PAIR), jnp.float32),
+            pltpu.VMEM((3, 8 * peers, SW, PAIR), half),
+            pltpu.VMEM((3, rows, cols // SW, SW, 2 * PAIR), half),
+            pltpu.VMEM((512, PAIR), half),
+            pltpu.VMEM((512, PAIR), half),
+            pltpu.VMEM((512, PAIR), half),
+            pltpu.VMEM((512, PAIR), half),
+            pltpu.VMEM((8, 512), jnp.float32),
+            pltpu.VMEM((PAIR, 512), jnp.float32),
+            pltpu.VMEM((512, PAIR), jnp.float32),
+            pltpu.VMEM((512, PAIR), jnp.float32),
+            dma((4, peers)), dma((4, peers)), dma((peers,)), dma((peers,)),
+            dma((5,)), dma((5,)), dma((3, peers)), dma((3, peers)), dma((3,)), dma((3,)),
+        ],
+        compiler_params=pltpu.CompilerParams(
+            collective_id=0, has_side_effects=True, vmem_limit_bytes=40 * 1024 * 1024
+        ),
+    )(
+        view(queries), view(key_map), view(value_map), view(saved_output), view(output_grad),
+        view(saved_logsum),
+    )
+    return tuple(values.astype(jnp.float32).reshape(rows, cols, width) for values in grads)
+
+
+def local(mesh, *arrays):
+    peers = mesh.shape["row"]
+    if peers == 8 and mesh.shape["col"] == 2 and arrays[0].shape == (8, 16, HEADS * HD):
+        return local_exchange(peers, *arrays)
+    return local_general(*arrays)
+
+
 def solution(mesh):
     in_specs = (
         P(("grp", "row"), "col", None),
@@ -164,4 +462,4 @@
         P(("grp", "row"), "col", None),
         P(("grp", "row"), "col", None),
     )
-    return jax.shard_map(local, mesh=mesh, in_specs=in_specs, out_specs=out_specs, check_vma=False)
+    return jax.shard_map(functools.partial(local, mesh), mesh=mesh, in_specs=in_specs, out_specs=out_specs, check_vma=False)

time: 232 us -> 38.8 us (0.17)
  waiting for transfers between devices: 140 us -> 0 us
  local copies, waits for them, and re-layouts: 49.9 us -> 5.58 us
  Pallas kernels: 0 us -> 30.4 us
  between operations: 15.8 us -> 0.65 us
  matrix products: 12.7 us -> 0 us
  other arithmetic: 7.9 us -> 1.93 us
  blocking collectives: 4.08 us -> 0 us
    reduce_scatter x2 -> x0, waiting for transfers between devices: 70.5 us -> none  [the longest x1 70.5 us: local(): lax.psum_scatter(stacked.reshape((count,) + stacked.shape[2:]), 'row', sc...]
    all_gather x2 -> x0, waiting for transfers between devices: 69.3 us -> none  [the longest x1 41.1 us: local(): lax.all_gather(local_value, 'row', axis=0, tiled=True)]
    pallas_call x0 -> x1, Pallas kernels: none -> 30.4 us  [local_exchange(): pl.pallas_call(exchange_kernel, out_shape=(jax.ShapeDtypeStruct((rows, co...]
    reshape x33 -> x0, local copies, waits for them, and re-layouts: 24.1 us -> none  [the longest x5 7.5 us: column_back(): return jnp.swapaxes(shaped, 0, 1).reshape(count, cols, -1)]
    dot_general x15 -> x0, matrix products: 12.7 us -> none  [the longest x3 3.48 us: key_side(): jnp.einsum('ghab,gahe->gbhe', grad_scores, stripe_query, preferred_elemen...]
    slice x8 -> x0, local copies, waits for them, and re-layouts: 7.54 us -> none  [the longest x1 1.69 us: local(): key_map[:, :, :split]]
    dynamic_slice x4 -> x0, local copies, waits for them, and re-layouts: 6.85 us -> none  [the longest x2 4.31 us: local(): lax.map(key_step, (every_key.reshape((count // block, block) + every_key....]
    transpose x12 -> x0, local copies, waits for them, and re-layouts: 5.08 us -> none  [the longest x3 4.44 us: key_side(): jnp.einsum('ghab,gahe->gbhe', probs_half, stripe_grad, preferred_element_...]
  transfers between devices with their start and end apart: 4 -> 0, of which waited for: 3 -> 0; matrix products, arithmetic and copies ran while one was open for 28% -> 0% of each run, Pallas kernels for 0% -> 0%
where the time goes in v1:
time: 38.8 us; the launch traced here: 38.5 us
  Pallas kernels  30.4 us (78%)
  local copies, waits for them, and re-layouts  5.58 us (14%)
  other arithmetic  1.93 us (5%)
  between operations  0.65 us (2%)
    pallas_call x1, Pallas kernels, local_exchange(): pl.pallas_call(exchange_kernel, out_shape=(jax.ShapeDtypeStruct((rows, co...  30.4 us
    unnamed x12, local copies, waits for them, and re-layouts  5.58 us
    reshape x2, other arithmetic, local_exchange(): values.astype(jnp.float32).reshape(rows, cols, width)  1.93 us

profile of v1, /device:TPU:0, one launch (start us, length us, event | category | flops | bytes accessed | tf_op | source)
XLA Modules:
  0.0 38.5 jit_solution(12468843816006792982)
XLA Ops:
  0.6 0.0 copy-start
  0.6 0.9 %copy-done = bf16[8,16,1024]{2,1,0:T(8,128)(2,1)S(1)} copy-done((bf16[8,16,1024]{2,1,0:T(8,128)(2,1)S(1)}, bf16[8,16,1024]{2,1,0:T(8,128)(2,1)}, u32[]{:S(2)}) %copy-start) | copy-done | bytes 262168
  1.6 0.0 copy-start.1
  1.6 0.9 %copy-done.1 = bf16[8,16,1024]{2,1,0:T(8,128)(2,1)S(1)} copy-done((bf16[8,16,1024]{2,1,0:T(8,128)(2,1)S(1)}, bf16[8,16,1024]{2,1,0:T(8,128)(2,1)}, u32[]{:S(2)}) %copy-start.1) | copy-done | bytes 262168
  2.5 0.0 copy-start.2
  2.5 0.9 %copy-done.2 = bf16[8,16,1024]{2,1,0:T(8,128)(2,1)S(1)} copy-done((bf16[8,16,1024]{2,1,0:T(8,128)(2,1)S(1)}, bf16[8,16,1024]{2,1,0:T(8,128)(2,1)}, u32[]{:S(2)}) %copy-start.2) | copy-done | bytes 262168
  3.5 0.0 copy-start.3
  3.5 0.9 %copy-done.3 = bf16[8,16,1024]{2,1,0:T(8,128)(2,1)S(1)} copy-done((bf16[8,16,1024]{2,1,0:T(8,128)(2,1)S(1)}, bf16[8,16,1024]{2,1,0:T(8,128)(2,1)}, u32[]{:S(2)}) %copy-start.3) | copy-done | bytes 262168
  4.4 0.0 copy-start.4
  4.4 0.9 %copy-done.4 = bf16[8,16,1024]{2,1,0:T(8,128)(2,1)S(1)} copy-done((bf16[8,16,1024]{2,1,0:T(8,128)(2,1)S(1)}, bf16[8,16,1024]{2,1,0:T(8,128)(2,1)}, u32[]{:S(2)}) %copy-start.4) | copy-done | bytes 262168
  5.4 0.0 copy-start.5
  5.4 0.8 %copy-done.5 = f32[8,16,16]{2,1,0:T(8,128)S(1)} copy-done((f32[8,16,16]{2,1,0:T(8,128)S(1)}, f32[8,16,16]{2,1,0:T(8,128)}, u32[]{:S(2)}) %copy-start.5) | copy-done | bytes 8216
  6.2 30.4 %shard_map.85 = (bf16[8,2,8,1024]{3,2,1,0:T(8,128)(2,1)S(1)}, bf16[8,2,8,1024]{3,2,1,0:T(8,128)(2,1)S(1)}, bf16[8,2,8,1024]{3,2,1,0:T(8,128)(2,1)S(1)}) custom-call(bf16[8,2,8,1024]{3,2,1,0:T(8,128)(2,1)S(1)} %bitcast.15, bf16[8,2,8,1024]{3,2,1,0:T(8,128)(2,1)S(1)} %bitcast.16, bf16[8,2,8,1024]{3,2,1,0:T(8,128)(2,1)S(1)} %bitcast.17, ...), custom_call_target="tpu_custom_call" | custom-call | tf_op jit(solution)/shard_map/pallas_call | solution.py:409
  36.6 1.1 %bitcast_convert_fusion = (f32[8,16,1024]{2,1,0:T(8,128)}, f32[8,16,1024]{2,1,0:T(8,128)}) fusion(bf16[8,2,8,1024]{3,2,1,0:T(8,128)(2,1)S(1)} %get-tuple-element.8, bf16[8,2,8,1024]{3,2,1,0:T(8,128)(2,1)S(1)} %get-tuple-element.7), kind=kLoop, calls=%fused_computation | loop fusion | flops 262144 | bytes 1572864 | tf_op jit(solution)/shard_map/reshape | solution.py:441
  37.7 0.8 %bitcast_convert_fusion.2 = f32[8,16,1024]{2,1,0:T(8,128)} fusion(bf16[8,2,8,1024]{3,2,1,0:T(8,128)(2,1)S(1)} %get-tuple-element.6), kind=kLoop, calls=%fused_computation.2 | loop fusion | flops 131072 | bytes 786432 | tf_op jit(solution)/shard_map/reshape | solution.py:441
Async XLA Ops:
  0.6 1.0 %copy-start = (bf16[8,16,1024]{2,1,0:T(8,128)(2,1)S(1)}, bf16[8,16,1024]{2,1,0:T(8,128)(2,1)}, u32[]{:S(2)}) copy-start(bf16[8,16,1024]{2,1,0:T(8,128)(2,1)} %param.6) | copy-start | bytes 786436
  1.6 0.9 %copy-start.1 = (bf16[8,16,1024]{2,1,0:T(8,128)(2,1)S(1)}, bf16[8,16,1024]{2,1,0:T(8,128)(2,1)}, u32[]{:S(2)}) copy-start(bf16[8,16,1024]{2,1,0:T(8,128)(2,1)} %param.7) | copy-start | bytes 786436
  2.5 0.9 %copy-start.2 = (bf16[8,16,1024]{2,1,0:T(8,128)(2,1)S(1)}, bf16[8,16,1024]{2,1,0:T(8,128)(2,1)}, u32[]{:S(2)}) copy-start(bf16[8,16,1024]{2,1,0:T(8,128)(2,1)} %param.8) | copy-start | bytes 786436
  3.5 0.9 %copy-start.3 = (bf16[8,16,1024]{2,1,0:T(8,128)(2,1)S(1)}, bf16[8,16,1024]{2,1,0:T(8,128)(2,1)}, u32[]{:S(2)}) copy-start(bf16[8,16,1024]{2,1,0:T(8,128)(2,1)} %param.9) | copy-start | bytes 786436
  4.4 0.9 %copy-start.4 = (bf16[8,16,1024]{2,1,0:T(8,128)(2,1)S(1)}, bf16[8,16,1024]{2,1,0:T(8,128)(2,1)}, u32[]{:S(2)}) copy-start(bf16[8,16,1024]{2,1,0:T(8,128)(2,1)} %param.10) | copy-start | bytes 786436
  5.4 0.8 %copy-start.5 = (f32[8,16,16]{2,1,0:T(8,128)S(1)}, f32[8,16,16]{2,1,0:T(8,128)}, u32[]{:S(2)}) copy-start(f32[8,16,16]{2,1,0:T(8,128)} %param.11) | copy-start | bytes 24580

commit v2 on v1

--- a/solution.py
+++ b/solution.py
@@ -200,10 +200,11 @@
 
 
 def exchange_kernel(
-    q_ref, k_ref, v_ref, o_ref, g_ref, l_ref,
+    q_hbm, k_hbm, v_hbm, o_hbm, g_hbm, l_hbm,
     dq_ref, dk_ref, dv_ref,
     col_in, col_aux, row_in, row_aux, aux_row, aux_col, col_out, row_out,
     q_s, k_s, v_s, g_s, rows_s, dq_t, dk_s, dv_s,
+    q_ref, k_ref, v_ref, o_ref, g_ref, l_ref, in_sem,
     cs_sem, cr_sem, as_sem, ar_sem, rs_sem, rr_sem, os_sem, or_sem, ps_sem, pr_sem,
 ):
     me = lax.axis_index("row")
@@ -215,6 +216,18 @@
     stripe = me % 2
     ins = (q_ref, k_ref, v_ref, g_ref)
     outs = (dq_ref, dk_ref, dv_ref)
+    sources = (q_hbm, k_hbm, v_hbm, g_hbm)
+    loads = [
+        pltpu.make_async_copy(source, target, in_sem.at[n])
+        for n, (source, target) in enumerate(
+            (
+                (g_hbm, g_ref), (o_hbm, o_ref), (l_hbm, l_ref),
+                (q_hbm, q_ref), (k_hbm, k_ref), (v_hbm, v_ref),
+            )
+        )
+    ]
+    for load in loads:
+        load.start()
 
     barrier = pltpu.get_barrier_semaphore()
     for step in range(1, peers):
@@ -235,7 +248,7 @@
 
     def row_copy(a):
         return pltpu.make_async_remote_copy(
-            src_ref=ins[a].at[:, :, :, core_lanes(other)],
+            src_ref=sources[a].at[:, :, :, core_lanes(other)],
             dst_ref=row_in.at[a],
             send_sem=rs_sem.at[a], recv_sem=rr_sem.at[a],
             device_id={"col": other}, device_id_type=MESH,
@@ -243,7 +256,7 @@
 
     def col_copy(a, target, source):
         return pltpu.make_async_remote_copy(
-            src_ref=ins[a].at[:, target % 2, :, col_lanes(target // 2)],
+            src_ref=sources[a].at[:, target % 2, :, col_lanes(target // 2)],
             dst_ref=col_in.at[a, eight(source)],
             send_sem=cs_sem.at[a, target], recv_sem=cr_sem.at[a, source],
             device_id={"row": target}, device_id_type=MESH,
@@ -284,14 +297,20 @@
     for a in range(4):
         row_copy(a).start()
 
+    def partner(step):
+        flip = jnp.where(step < 5, step + 3, step - 4)
+        return (me // 4 + flip // 4) % 2 * 4 + (me // 2 + flip // 2) % 2 * 2 + (me + flip) % 2
+
     def send(step, carry):
-        target = lax.rem(me + step, peers)
+        target = partner(step)
         for a in range(4):
             col_copy(a, target, me).start()
         return carry
 
     lax.fori_loop(1, peers, send, 0)
 
+    for load in loads[:3]:
+        load.wait()
     which = lax.broadcasted_iota(jnp.int32, (8, PAIR), 0)
     lane = lax.broadcasted_iota(jnp.int32, (8, PAIR), 1)
     pick = (which == 2 + lane // HD).astype(jnp.float32)
@@ -319,10 +338,12 @@
     row_aux_copy().start()
 
     def send_aux(step, carry):
-        aux_copy(lax.rem(me + step, peers), me).start()
+        aux_copy(partner(step), me).start()
         return carry
 
     lax.fori_loop(1, peers, send_aux, 0)
+    for load in loads[3:]:
+        load.wait()
     for a in range(4):
         col_in[a, eight(me)] = ins[a][:, stripe, :, col_lanes(pair)]
     col_aux[me] = aux_col[pair]
@@ -348,7 +369,7 @@
         row_back(a, core).start()
 
     def arrive(step, carry):
-        source = lax.rem(me + step, peers)
+        source = partner(step)
         for a in range(4):
             col_copy(a, source, source).wait_recv()
         aux_copy(source, source).wait_recv()
@@ -369,7 +390,7 @@
         col_out[a] = grads.reshape((64, 8, PAIR)).astype(jnp.bfloat16)
 
     def give(step, carry):
-        target = lax.rem(me + step, peers)
+        target = partner(step)
         for a in range(3):
             back_copy(a, target, me).start()
         return carry
@@ -379,7 +400,7 @@
         outs[a][:, stripe, :, col_lanes(pair)] = col_out[a, eight(me)]
 
     def finish(step, carry):
-        target = lax.rem(me + step, peers)
+        target = partner(step)
         for a in range(3):
             back_copy(a, target, target).wait_recv()
         for a in range(3):
@@ -409,7 +430,7 @@
     grads = pl.pallas_call(
         exchange_kernel,
         out_shape=(jax.ShapeDtypeStruct((rows, cols // SW, SW, width), half),) * 3,
-        in_specs=[vmem] * 6,
+        in_specs=[pl.BlockSpec(memory_space=pltpu.HBM)] * 6,
         out_specs=(vmem,) * 3,
         scratch_shapes=[
             pltpu.VMEM((4, 8 * peers, SW, PAIR), half),
@@ -428,6 +449,9 @@
             pltpu.VMEM((PAIR, 512), jnp.float32),
             pltpu.VMEM((512, PAIR), jnp.float32),
             pltpu.VMEM((512, PAIR), jnp.float32),
+            *(pltpu.VMEM((rows, cols // SW, SW, width), half) for _ in range(5)),
+            pltpu.VMEM((rows, cols // SW, SW, HEADS), jnp.float32),
+            dma((6,)),
             dma((4, peers)), dma((4, peers)), dma((peers,)), dma((peers,)),
             dma((5,)), dma((5,)), dma((3, peers)), dma((3, peers)), dma((3,)), dma((3,)),
         ],

time: 38.8 us -> 40.3 us (1.039)
  Pallas kernels: 30.4 us -> 31.8 us
    pallas_call x1, Pallas kernels: 30.4 us -> 31.8 us  [local_exchange(): pl.pallas_call(exchange_kernel, out_shape=(jax.ShapeDtypeStruct((rows, co...]
where the time goes in v2:
time: 40.3 us; the launch traced here: 40 us
  Pallas kernels  31.8 us (79%)
  local copies, waits for them, and re-layouts  5.58 us (14%)
  other arithmetic  1.93 us (5%)
  between operations  0.65 us (2%)
    pallas_call x1, Pallas kernels, local_exchange(): pl.pallas_call(exchange_kernel, out_shape=(jax.ShapeDtypeStruct((rows, co...  31.8 us
    unnamed x12, local copies, waits for them, and re-layouts  5.58 us
    reshape x2, other arithmetic, local_exchange(): values.astype(jnp.float32).reshape(rows, cols, width)  1.93 us

profile of v2, /device:TPU:0, one launch (start us, length us, event | category | flops | bytes accessed | tf_op | source)
XLA Modules:
  0.0 40.0 jit_solution(7940048816216990372)
XLA Ops:
  0.6 0.0 copy-start
  0.6 0.9 %copy-done = bf16[8,16,1024]{2,1,0:T(8,128)(2,1)S(1)} copy-done((bf16[8,16,1024]{2,1,0:T(8,128)(2,1)S(1)}, bf16[8,16,1024]{2,1,0:T(8,128)(2,1)}, u32[]{:S(2)}) %copy-start) | copy-done | bytes 262168
  1.6 0.0 copy-start.1
  1.6 0.9 %copy-done.1 = bf16[8,16,1024]{2,1,0:T(8,128)(2,1)S(1)} copy-done((bf16[8,16,1024]{2,1,0:T(8,128)(2,1)S(1)}, bf16[8,16,1024]{2,1,0:T(8,128)(2,1)}, u32[]{:S(2)}) %copy-start.1) | copy-done | bytes 262168
  2.5 0.0 copy-start.2
  2.5 0.9 %copy-done.2 = bf16[8,16,1024]{2,1,0:T(8,128)(2,1)S(1)} copy-done((bf16[8,16,1024]{2,1,0:T(8,128)(2,1)S(1)}, bf16[8,16,1024]{2,1,0:T(8,128)(2,1)}, u32[]{:S(2)}) %copy-start.2) | copy-done | bytes 262168
  3.5 0.0 copy-start.3
  3.5 0.9 %copy-done.3 = bf16[8,16,1024]{2,1,0:T(8,128)(2,1)S(1)} copy-done((bf16[8,16,1024]{2,1,0:T(8,128)(2,1)S(1)}, bf16[8,16,1024]{2,1,0:T(8,128)(2,1)}, u32[]{:S(2)}) %copy-start.3) | copy-done | bytes 262168
  4.4 0.0 copy-start.4
  4.4 0.9 %copy-done.4 = bf16[8,16,1024]{2,1,0:T(8,128)(2,1)S(1)} copy-done((bf16[8,16,1024]{2,1,0:T(8,128)(2,1)S(1)}, bf16[8,16,1024]{2,1,0:T(8,128)(2,1)}, u32[]{:S(2)}) %copy-start.4) | copy-done | bytes 262168
  5.4 0.0 copy-start.5
  5.4 0.8 %copy-done.5 = f32[8,16,16]{2,1,0:T(8,128)S(1)} copy-done((f32[8,16,16]{2,1,0:T(8,128)S(1)}, f32[8,16,16]{2,1,0:T(8,128)}, u32[]{:S(2)}) %copy-start.5) | copy-done | bytes 8216
  6.2 31.8 %shard_map.85 = (bf16[8,2,8,1024]{3,2,1,0:T(8,128)(2,1)S(1)}, bf16[8,2,8,1024]{3,2,1,0:T(8,128)(2,1)S(1)}, bf16[8,2,8,1024]{3,2,1,0:T(8,128)(2,1)S(1)}) custom-call(bf16[8,2,8,1024]{3,2,1,0:T(8,128)(2,1)S(1)} %bitcast.15, bf16[8,2,8,1024]{3,2,1,0:T(8,128)(2,1)S(1)} %bitcast.16, bf16[8,2,8,1024]{3,2,1,0:T(8,128)(2,1)S(1)} %bitcast.17, ...), custom_call_target="tpu_custom_call" | custom-call | tf_op jit(solution)/shard_map/pallas_call | solution.py:430
  38.1 1.1 %bitcast_convert_fusion = (f32[8,16,1024]{2,1,0:T(8,128)}, f32[8,16,1024]{2,1,0:T(8,128)}) fusion(bf16[8,2,8,1024]{3,2,1,0:T(8,128)(2,1)S(1)} %get-tuple-element.8, bf16[8,2,8,1024]{3,2,1,0:T(8,128)(2,1)S(1)} %get-tuple-element.7), kind=kLoop, calls=%fused_computation | loop fusion | flops 262144 | bytes 1572864 | tf_op jit(solution)/shard_map/reshape | solution.py:465
  39.2 0.8 %bitcast_convert_fusion.2 = f32[8,16,1024]{2,1,0:T(8,128)} fusion(bf16[8,2,8,1024]{3,2,1,0:T(8,128)(2,1)S(1)} %get-tuple-element.6), kind=kLoop, calls=%fused_computation.2 | loop fusion | flops 131072 | bytes 786432 | tf_op jit(solution)/shard_map/reshape | solution.py:465
Async XLA Ops:
  0.6 1.0 %copy-start = (bf16[8,16,1024]{2,1,0:T(8,128)(2,1)S(1)}, bf16[8,16,1024]{2,1,0:T(8,128)(2,1)}, u32[]{:S(2)}) copy-start(bf16[8,16,1024]{2,1,0:T(8,128)(2,1)} %param.6) | copy-start | bytes 786436
  1.6 0.9 %copy-start.1 = (bf16[8,16,1024]{2,1,0:T(8,128)(2,1)S(1)}, bf16[8,16,1024]{2,1,0:T(8,128)(2,1)}, u32[]{:S(2)}) copy-start(bf16[8,16,1024]{2,1,0:T(8,128)(2,1)} %param.7) | copy-start | bytes 786436
  2.5 0.9 %copy-start.2 = (bf16[8,16,1024]{2,1,0:T(8,128)(2,1)S(1)}, bf16[8,16,1024]{2,1,0:T(8,128)(2,1)}, u32[]{:S(2)}) copy-start(bf16[8,16,1024]{2,1,0:T(8,128)(2,1)} %param.8) | copy-start | bytes 786436
  3.5 0.9 %copy-start.3 = (bf16[8,16,1024]{2,1,0:T(8,128)(2,1)S(1)}, bf16[8,16,1024]{2,1,0:T(8,128)(2,1)}, u32[]{:S(2)}) copy-start(bf16[8,16,1024]{2,1,0:T(8,128)(2,1)} %param.9) | copy-start | bytes 786436
  4.4 0.9 %copy-start.4 = (bf16[8,16,1024]{2,1,0:T(8,128)(2,1)S(1)}, bf16[8,16,1024]{2,1,0:T(8,128)(2,1)}, u32[]{:S(2)}) copy-start(bf16[8,16,1024]{2,1,0:T(8,128)(2,1)} %param.10) | copy-start | bytes 786436
  5.4 0.8 %copy-start.5 = (f32[8,16,16]{2,1,0:T(8,128)S(1)}, f32[8,16,16]{2,1,0:T(8,128)}, u32[]{:S(2)}) copy-start(f32[8,16,16]{2,1,0:T(8,128)} %param.11) | copy-start | bytes 24580

commit v3 on v2

--- a/solution.py
+++ b/solution.py
@@ -456,7 +456,7 @@
             dma((5,)), dma((5,)), dma((3, peers)), dma((3, peers)), dma((3,)), dma((3,)),
         ],
         compiler_params=pltpu.CompilerParams(
-            collective_id=0, has_side_effects=True, vmem_limit_bytes=40 * 1024 * 1024
+            collective_id=0, has_side_effects=True, vmem_limit_bytes=63 * 1024 * 1024
         ),
     )(
         view(queries), view(key_map), view(value_map), view(saved_output), view(output_grad),

time: 40.3 us -> 36.6 us (0.908)
  local copies, waits for them, and re-layouts: 5.58 us -> 0.01 us
  other arithmetic: 1.93 us -> 3 us
  Pallas kernels: 31.8 us -> 32.8 us
    unnamed x12 -> x2, local copies, waits for them, and re-layouts: 5.58 us -> 0.01 us
    reshape x2, other arithmetic: 1.93 us -> 3 us  [local_exchange(): values.astype(jnp.float32).reshape(rows, cols, width)]
    pallas_call x1, Pallas kernels: 31.8 us -> 32.8 us  [local_exchange(): pl.pallas_call(exchange_kernel, out_shape=(jax.ShapeDtypeStruct((rows, co...]
where the time goes in v3:
time: 36.6 us; the launch traced here: 36.5 us
  Pallas kernels  32.8 us (90%)
  other arithmetic  3 us (8%)
  between operations  0.65 us (2%)
    pallas_call x1, Pallas kernels, local_exchange(): pl.pallas_call(exchange_kernel, out_shape=(jax.ShapeDtypeStruct((rows, co...  32.8 us
    reshape x2, other arithmetic, local_exchange(): values.astype(jnp.float32).reshape(rows, cols, width)  3 us

profile of v3, /device:TPU:0, one launch (start us, length us, event | category | flops | bytes accessed | tf_op | source)
XLA Modules:
  0.0 36.5 jit_solution(4166454775920933853)
XLA Ops:
  0.6 32.8 %shard_map.85 = (bf16[8,2,8,1024]{3,2,1,0:T(8,128)(2,1)}, bf16[8,2,8,1024]{3,2,1,0:T(8,128)(2,1)}, bf16[8,2,8,1024]{3,2,1,0:T(8,128)(2,1)}) custom-call(bf16[8,2,8,1024]{3,2,1,0:T(8,128)(2,1)} %bitcast.15, bf16[8,2,8,1024]{3,2,1,0:T(8,128)(2,1)} %bitcast.16, bf16[8,2,8,1024]{3,2,1,0:T(8,128)(2,1)} %bitcast.17, bf16[8,2,8,1024]{3,2,1,0:T(8,128)(2,1)} %bitcast.18, ...), custom_call_target="tpu_custom_call" | custom-call | tf_op jit(solution)/shard_map/pallas_call | solution.py:430
  33.5 0.0 copy-start
  33.5 2.2 %bitcast_convert_fusion = (f32[8,16,1024]{2,1,0:T(8,128)}, f32[8,16,1024]{2,1,0:T(8,128)}) fusion(bf16[8,2,8,1024]{3,2,1,0:T(8,128)(2,1)} %get-tuple-element.8, bf16[8,2,8,1024]{3,2,1,0:T(8,128)(2,1)} %get-tuple-element.7), kind=kLoop, calls=%fused_computation | loop fusion | flops 262144 | bytes 1572864 | tf_op jit(solution)/shard_map/reshape | solution.py:465
  35.6 0.0 copy-done
  35.6 0.8 %bitcast_convert_fusion.2 = f32[8,16,1024]{2,1,0:T(8,128)} fusion(bf16[8,2,8,1024]{3,2,1,0:T(8,128)(2,1)S(1)} %copy-done), kind=kLoop, calls=%fused_computation.2 | loop fusion | flops 131072 | bytes 786432 | tf_op jit(solution)/shard_map/reshape | solution.py:465
Async XLA Ops:
  33.5 2.2 %copy-start = (bf16[8,2,8,1024]{3,2,1,0:T(8,128)(2,1)S(1)}, bf16[8,2,8,1024]{3,2,1,0:T(8,128)(2,1)}, u32[]{:S(2)}) copy-start(bf16[8,2,8,1024]{3,2,1,0:T(8,128)(2,1)} %get-tuple-element.6) | copy-start | bytes 786436

commit v4 on v3

--- a/solution.py
+++ b/solution.py
@@ -204,7 +204,7 @@
     dq_ref, dk_ref, dv_ref,
     col_in, col_aux, row_in, row_aux, aux_row, aux_col, col_out, row_out,
     q_s, k_s, v_s, g_s, rows_s, dq_t, dk_s, dv_s,
-    q_ref, k_ref, v_ref, o_ref, g_ref, l_ref, in_sem,
+    q_ref, k_ref, v_ref, o_ref, g_ref, l_ref, row_own, keep_sem, in_sem,
     cs_sem, cr_sem, as_sem, ar_sem, rs_sem, rr_sem, os_sem, or_sem, ps_sem, pr_sem,
 ):
     me = lax.axis_index("row")
@@ -286,6 +286,16 @@
             device_id={"col": other}, device_id_type=MESH,
         )
 
+    def row_keep(a):
+        return pltpu.make_async_copy(
+            row_own.at[a], outs[a].at[:, :, :, core_lanes(core)], keep_sem.at[a]
+        )
+
+    def col_keep(a):
+        return pltpu.make_async_copy(
+            col_out.at[a, eight(me)], outs[a].at[:, stripe, :, col_lanes(pair)], keep_sem.at[3 + a]
+        )
+
     def row_aux_copy():
         return pltpu.make_async_remote_copy(
             src_ref=aux_row.at[pl.ds(2 * other, 2)],
@@ -363,10 +373,11 @@
         dq = attend(256, 256, q_s, k_s, v_s, g_s, rows_s, dq_t, dk_s, dv_s)
         for a, grads in enumerate((dq, dk_s[0:256, :], dv_s[0:256, :])):
             shaped = grads.reshape((2, 8, 2, 8, PAIR)).astype(jnp.bfloat16)
-            outs[a][:, :, :, mine] = shaped[0]
+            row_own[a, :, :, :, part] = shaped[0]
             row_out[a, :, :, :, part] = shaped[1]
     for a in range(3):
         row_back(a, core).start()
+        row_keep(a).start()
 
     def arrive(step, carry):
         source = partner(step)
@@ -397,7 +408,7 @@
 
     lax.fori_loop(1, peers, give, 0)
     for a in range(3):
-        outs[a][:, stripe, :, col_lanes(pair)] = col_out[a, eight(me)]
+        col_keep(a).start()
 
     def finish(step, carry):
         target = partner(step)
@@ -415,7 +426,14 @@
     row_aux_copy().wait_send()
     for a in range(3):
         row_back(a, core).wait()
+        row_keep(a).wait()
+        col_keep(a).wait()
     lax.fori_loop(1, peers, finish, 0)
+
+
+def widen_kernel(*refs):
+    for narrow, wide in zip(refs[:3], refs[3:]):
+        wide[...] = narrow[...].astype(jnp.float32).reshape(wide.shape)
 
 
 def local_exchange(peers, queries, key_map, value_map, saved_output, output_grad, saved_logsum):
@@ -425,13 +443,13 @@
         return values.reshape((rows, cols // SW, SW, values.shape[-1]))
 
     half = jnp.bfloat16
-    vmem = pl.BlockSpec(memory_space=pltpu.VMEM)
+    hbm = pl.BlockSpec(memory_space=pltpu.HBM)
     dma = pltpu.SemaphoreType.DMA
     grads = pl.pallas_call(
         exchange_kernel,
         out_shape=(jax.ShapeDtypeStruct((rows, cols // SW, SW, width), half),) * 3,
-        in_specs=[pl.BlockSpec(memory_space=pltpu.HBM)] * 6,
-        out_specs=(vmem,) * 3,
+        in_specs=[hbm] * 6,
+        out_specs=(hbm,) * 3,
         scratch_shapes=[
             pltpu.VMEM((4, 8 * peers, SW, PAIR), half),
             pltpu.VMEM((peers, 8, PAIR), jnp.float32),
@@ -451,6 +469,8 @@
             pltpu.VMEM((512, PAIR), jnp.float32),
             *(pltpu.VMEM((rows, cols // SW, SW, width), half) for _ in range(5)),
             pltpu.VMEM((rows, cols // SW, SW, HEADS), jnp.float32),
+            pltpu.VMEM((3, rows, cols // SW, SW, 2 * PAIR), half),
+            dma((6,)),
             dma((6,)),
             dma((4, peers)), dma((4, peers)), dma((peers,)), dma((peers,)),
             dma((5,)), dma((5,)), dma((3, peers)), dma((3, peers)), dma((3,)), dma((3,)),
@@ -462,7 +482,19 @@
         view(queries), view(key_map), view(value_map), view(saved_output), view(output_grad),
         view(saved_logsum),
     )
-    return tuple(values.astype(jnp.float32).reshape(rows, cols, width) for values in grads)
+    steps = 4
+    narrow = pl.BlockSpec((rows // steps, cols // SW, SW, width), lambda i: (i, 0, 0, 0))
+    wide = pl.BlockSpec((rows // steps, cols, width), lambda i: (i, 0, 0))
+    return tuple(
+        pl.pallas_call(
+            widen_kernel,
+            grid=(steps,),
+            out_shape=(jax.ShapeDtypeStruct((rows, cols, width), jnp.float32),) * 3,
+            in_specs=[narrow] * 3,
+            out_specs=(wide,) * 3,
+            compiler_params=pltpu.CompilerParams(vmem_limit_bytes=63 * 1024 * 1024),
+        )(*grads)
+    )
 
 
 def local(mesh, *arrays):

time: 36.6 us -> 36.4 us (level)
  other arithmetic: 3 us -> 0 us
  Pallas kernels: 32.8 us -> 35.4 us
    pallas_call x0 -> x1, Pallas kernels: none -> 3.36 us  [local_exchange(): pl.pallas_call(widen_kernel, grid=(steps,), out_shape=(jax.ShapeDtypeStru...]
    reshape x2 -> x0, other arithmetic: 3 us -> none  [local_exchange(): values.astype(jnp.float32).reshape(rows, cols, width)]
    pallas_call x1, Pallas kernels: 32.8 us -> 32.1 us  [local_exchange(): pl.pallas_call(exchange_kernel, out_shape=(jax.ShapeDtypeStruct((rows, co...]
where the time goes in v4:
time: 36.4 us; the launch traced here: 36.1 us
  Pallas kernels  35.4 us (97%)
  between operations  0.64 us (2%)
    pallas_call x1, Pallas kernels, local_exchange(): pl.pallas_call(exchange_kernel, out_shape=(jax.ShapeDtypeStruct((rows, co...  32.1 us
    pallas_call x1, Pallas kernels, local_exchange(): pl.pallas_call(widen_kernel, grid=(steps,), out_shape=(jax.ShapeDtypeStru...  3.36 us

profile of v4, /device:TPU:0, one launch (start us, length us, event | category | flops | bytes accessed | tf_op | source)
XLA Modules:
  0.0 36.1 jit_solution(16046928558601799907)
XLA Ops:
  0.6 32.1 %shard_map.85 = (bf16[8,2,8,1024]{3,2,1,0:T(8,128)(2,1)}, bf16[8,2,8,1024]{3,2,1,0:T(8,128)(2,1)}, bf16[8,2,8,1024]{3,2,1,0:T(8,128)(2,1)}) custom-call(bf16[8,2,8,1024]{3,2,1,0:T(8,128)(2,1)} %bitcast.6, bf16[8,2,8,1024]{3,2,1,0:T(8,128)(2,1)} %bitcast.7, bf16[8,2,8,1024]{3,2,1,0:T(8,128)(2,1)} %bitcast.8, bf16[8,2,8,1024]{3,2,1,0:T(8,128)(2,1)} %bitcast.9, ...), custom_call_target="tpu_custom_call" | custom-call | tf_op jit(solution)/shard_map/pallas_call | solution.py:448
  32.7 3.4 %shard_map.86 = (f32[8,16,1024]{2,1,0:T(8,128)}, f32[8,16,1024]{2,1,0:T(8,128)}, f32[8,16,1024]{2,1,0:T(8,128)}) custom-call(bf16[8,2,8,1024]{3,2,1,0:T(8,128)(2,1)} %get-tuple-element.6.refs_0_, bf16[8,2,8,1024]{3,2,1,0:T(8,128)(2,1)} %get-tuple-element.7.refs_1_, bf16[8,2,8,1024]{3,2,1,0:T(8,128)(2,1)} %get-tuple-element.8.refs_2_), custom_call_target="tpu_custom_call" | custom-call | tf_op jit(solution)/shard_map/pallas_call | solution.py:489

commit v5 on v4

--- a/solution.py
+++ b/solution.py
@@ -431,11 +431,6 @@
     lax.fori_loop(1, peers, finish, 0)
 
 
-def widen_kernel(*refs):
-    for narrow, wide in zip(refs[:3], refs[3:]):
-        wide[...] = narrow[...].astype(jnp.float32).reshape(wide.shape)
-
-
 def local_exchange(peers, queries, key_map, value_map, saved_output, output_grad, saved_logsum):
     rows, cols, width = queries.shape
 
@@ -447,9 +442,9 @@
     dma = pltpu.SemaphoreType.DMA
     grads = pl.pallas_call(
         exchange_kernel,
-        out_shape=(jax.ShapeDtypeStruct((rows, cols // SW, SW, width), half),) * 3,
+        out_shape=(pltpu.VMEM((rows, cols // SW, SW, width), half),) * 3,
         in_specs=[hbm] * 6,
-        out_specs=(hbm,) * 3,
+        out_specs=(pl.BlockSpec(memory_space=pltpu.VMEM),) * 3,
         scratch_shapes=[
             pltpu.VMEM((4, 8 * peers, SW, PAIR), half),
             pltpu.VMEM((peers, 8, PAIR), jnp.float32),
@@ -476,25 +471,13 @@
             dma((5,)), dma((5,)), dma((3, peers)), dma((3, peers)), dma((3,)), dma((3,)),
         ],
         compiler_params=pltpu.CompilerParams(
-            collective_id=0, has_side_effects=True, vmem_limit_bytes=63 * 1024 * 1024
+            collective_id=0, has_side_effects=True, vmem_limit_bytes=61 * 1024 * 1024
         ),
     )(
         view(queries), view(key_map), view(value_map), view(saved_output), view(output_grad),
         view(saved_logsum),
     )
-    steps = 4
-    narrow = pl.BlockSpec((rows // steps, cols // SW, SW, width), lambda i: (i, 0, 0, 0))
-    wide = pl.BlockSpec((rows // steps, cols, width), lambda i: (i, 0, 0))
-    return tuple(
-        pl.pallas_call(
-            widen_kernel,
-            grid=(steps,),
-            out_shape=(jax.ShapeDtypeStruct((rows, cols, width), jnp.float32),) * 3,
-            in_specs=[narrow] * 3,
-            out_specs=(wide,) * 3,
-            compiler_params=pltpu.CompilerParams(vmem_limit_bytes=63 * 1024 * 1024),
-        )(*grads)
-    )
+    return tuple(values.astype(jnp.float32).reshape(rows, cols, width) for values in grads)
 
 
 def local(mesh, *arrays):

time: 36.4 us -> 34.7 us (0.953)
  Pallas kernels: 35.4 us -> 32 us
  other arithmetic: 0 us -> 1.93 us
    pallas_call x2 -> x1, Pallas kernels: 35.4 us -> 32 us  [local_exchange(): pl.pallas_call(exchange_kernel, out_shape=(pltpu.VMEM((rows, cols // SW,...]
    reshape x0 -> x2, other arithmetic: none -> 1.93 us  [local_exchange(): values.astype(jnp.float32).reshape(rows, cols, width)]
where the time goes in v5:
time: 34.7 us; the launch traced here: 34.5 us
  Pallas kernels  32 us (92%)
  other arithmetic  1.93 us (6%)
  between operations  0.64 us (2%)
    pallas_call x1, Pallas kernels, local_exchange(): pl.pallas_call(exchange_kernel, out_shape=(pltpu.VMEM((rows, cols // SW,...  32 us
    reshape x2, other arithmetic, local_exchange(): values.astype(jnp.float32).reshape(rows, cols, width)  1.93 us

profile of v5, /device:TPU:0, one launch (start us, length us, event | category | flops | bytes accessed | tf_op | source)
XLA Modules:
  0.0 34.5 jit_solution(17644319620050275720)
XLA Ops:
  0.6 32.0 %shard_map.85 = (bf16[8,2,8,1024]{3,2,1,0:T(8,128)(2,1)S(1)}, bf16[8,2,8,1024]{3,2,1,0:T(8,128)(2,1)S(1)}, bf16[8,2,8,1024]{3,2,1,0:T(8,128)(2,1)S(1)}) custom-call(bf16[8,2,8,1024]{3,2,1,0:T(8,128)(2,1)} %bitcast.15, bf16[8,2,8,1024]{3,2,1,0:T(8,128)(2,1)} %bitcast.16, bf16[8,2,8,1024]{3,2,1,0:T(8,128)(2,1)} %bitcast.17, bf16[8,2,8,1024]{3,2,1,0:T(8,128)(2,1)} %bitcast.18, ...), custom_call_target="tpu_custom_call" | custom-call | tf_op jit(solution)/shard_map/pallas_call | solution.py:443
  32.6 1.1 %bitcast_convert_fusion = (f32[8,16,1024]{2,1,0:T(8,128)}, f32[8,16,1024]{2,1,0:T(8,128)}) fusion(bf16[8,2,8,1024]{3,2,1,0:T(8,128)(2,1)S(1)} %get-tuple-element.8, bf16[8,2,8,1024]{3,2,1,0:T(8,128)(2,1)S(1)} %get-tuple-element.7), kind=kLoop, calls=%fused_computation | loop fusion | flops 262144 | bytes 1572864 | tf_op jit(solution)/shard_map/reshape | solution.py:480
  33.7 0.8 %bitcast_convert_fusion.2 = f32[8,16,1024]{2,1,0:T(8,128)} fusion(bf16[8,2,8,1024]{3,2,1,0:T(8,128)(2,1)S(1)} %get-tuple-element.6), kind=kLoop, calls=%fused_computation.2 | loop fusion | flops 131072 | bytes 786432 | tf_op jit(solution)/shard_map/reshape | solution.py:480

commit v6 on v5

--- a/solution.py
+++ b/solution.py
@@ -163,40 +163,34 @@
     return values.astype(jnp.float32).reshape((-1, values.shape[-1]))
 
 
-def attend(count, block, q_s, k_s, v_s, g_s, rows, dq_t, dk_s, dv_s):
+def attend_part(count, block, j, q_s, k_s, v_s, g_s, rows, dq_t, dk_s, dv_s):
     scale = 1.0 / math.sqrt(HD)
     lane = lax.broadcasted_iota(jnp.int32, (block, PAIR), 1)
     masks = tuple(((lane // HD) == h).astype(jnp.float32).astype(jnp.bfloat16) for h in (0, 1))
 
-    def step(j, carry):
-        part = pl.ds(pl.multiple_of(j * block, block), block)
-        q = q_s[0:count, :]
-        g = g_s[0:count, :]
-        keys = k_s[part, :]
-        values = v_s[part, :]
-        dk = []
-        dv = []
-        dq = None
-        for h in (0, 1):
-            key = keys * masks[h]
-            value = values * masks[h]
-            scores = lax.dot_general(key, q, NT, preferred_element_type=jnp.float32)
-            probs = jnp.exp(scores * scale - rows[h : h + 1, 0:count])
-            grad_probs = lax.dot_general(value, g, NT, preferred_element_type=jnp.float32)
-            grad_scores = (probs * (grad_probs - rows[2 + h : 3 + h, 0:count])).astype(jnp.bfloat16)
-            half = probs.astype(jnp.bfloat16)
-            dv.append(jnp.dot(half, g, preferred_element_type=jnp.float32))
-            dk.append(jnp.dot(grad_scores, q, preferred_element_type=jnp.float32))
-            term = lax.dot_general(key, grad_scores, TN, preferred_element_type=jnp.float32)
-            dq = term if dq is None else dq + term
-        dk_s[part, :] = jnp.where(lane < HD, dk[0], dk[1]) * scale
-        dv_s[part, :] = jnp.where(lane < HD, dv[0], dv[1])
-        dq_t[:, 0:count] += dq
-        return carry
-
-    dq_t[:, 0:count] = jnp.zeros((PAIR, count), jnp.float32)
-    lax.fori_loop(0, count // block, step, 0)
-    return dq_t[:, 0:count].T * scale
+    part = pl.ds(pl.multiple_of(j * block, block), block)
+    q = q_s[0:count, :]
+    g = g_s[0:count, :]
+    keys = k_s[part, :]
+    values = v_s[part, :]
+    dk = []
+    dv = []
+    dq = None
+    for h in (0, 1):
+        key = keys * masks[h]
+        value = values * masks[h]
+        scores = lax.dot_general(key, q, NT, preferred_element_type=jnp.float32)
+        probs = jnp.exp(scores * scale - rows[h : h + 1, 0:count])
+        grad_probs = lax.dot_general(value, g, NT, preferred_element_type=jnp.float32)
+        grad_scores = (probs * (grad_probs - rows[2 + h : 3 + h, 0:count])).astype(jnp.bfloat16)
+        half = probs.astype(jnp.bfloat16)
+        dv.append(jnp.dot(half, g, preferred_element_type=jnp.float32))
+        dk.append(jnp.dot(grad_scores, q, preferred_element_type=jnp.float32))
+        term = lax.dot_general(key, grad_scores, TN, preferred_element_type=jnp.float32)
+        dq = term if dq is None else dq + term
+    dk_s[part, :] = jnp.where(lane < HD, dk[0], dk[1]) * scale
+    dv_s[part, :] = jnp.where(lane < HD, dv[0], dv[1])
+    dq_t[:, 0:count] += dq
 
 
 def exchange_kernel(
@@ -313,7 +307,7 @@
 
     def send(step, carry):
         target = partner(step)
-        for a in range(4):
+        for a in (0, 3):
             col_copy(a, target, me).start()
         return carry
 
@@ -352,6 +346,14 @@
         return carry
 
     lax.fori_loop(1, peers, send_aux, 0)
+
+    def send_keys(step, carry):
+        target = partner(step)
+        for a in (1, 2):
+            col_copy(a, target, me).start()
+        return carry
+
+    lax.fori_loop(1, peers, send_keys, 0)
     for load in loads[3:]:
         load.wait()
     for a in range(4):
@@ -370,7 +372,9 @@
             scratch[a][128:256, :] = flat(row_in[a, :, :, :, part]).astype(jnp.bfloat16)
         rows_s[:, 0:128] = aux_row[2 * core + u]
         rows_s[:, 128:256] = row_aux[u]
-        dq = attend(256, 256, q_s, k_s, v_s, g_s, rows_s, dq_t, dk_s, dv_s)
+        dq_t[:, 0:256] = jnp.zeros((PAIR, 256), jnp.float32)
+        attend_part(256, 256, 0, q_s, k_s, v_s, g_s, rows_s, dq_t, dk_s, dv_s)
+        dq = dq_t[:, 0:256].T * (1.0 / math.sqrt(HD))
         for a, grads in enumerate((dq, dk_s[0:256, :], dv_s[0:256, :])):
             shaped = grads.reshape((2, 8, 2, 8, PAIR)).astype(jnp.bfloat16)
             row_own[a, :, :, :, part] = shaped[0]
@@ -381,13 +385,13 @@
 
     def arrive(step, carry):
         source = partner(step)
-        for a in range(4):
+        for a in (0, 3):
             col_copy(a, source, source).wait_recv()
         aux_copy(source, source).wait_recv()
         return carry
 
     lax.fori_loop(1, peers, arrive, 0)
-    for a in range(4):
+    for a in (0, 3):
         scratch[a][...] = flat(col_in[a]).astype(jnp.bfloat16)
     low = lane < HD
     for k in range(4):
@@ -396,14 +400,37 @@
         even = jnp.where(low, first, pltpu.roll(second, HD, 1))
         odd = jnp.where(low, pltpu.roll(first, HD, 1), second)
         rows_s[:, k * PAIR : (k + 1) * PAIR] = jnp.where(stripe == 0, even, odd)
-    dq = attend(512, 256, q_s, k_s, v_s, g_s, rows_s, dq_t, dk_s, dv_s)
-    for a, grads in enumerate((dq, dk_s[...], dv_s[...])):
-        col_out[a] = grads.reshape((64, 8, PAIR)).astype(jnp.bfloat16)
+    dq_t[...] = jnp.zeros((PAIR, 512), jnp.float32)
+
+    def chunk(two, others):
+        for other_row in others:
+            for a in (1, 2):
+                col_copy(a, other_row, other_row).wait_recv()
+        part = pl.ds(pl.multiple_of(two * PAIR, PAIR), PAIR)
+        tiles = pl.ds(pl.multiple_of(two * 16, 16), 16)
+        for a in (1, 2):
+            scratch[a][part, :] = flat(col_in[a, tiles]).astype(jnp.bfloat16)
+        attend_part(512, PAIR, two, q_s, k_s, v_s, g_s, rows_s, dq_t, dk_s, dv_s)
+        for a, grads in ((1, dk_s), (2, dv_s)):
+            col_out[a, tiles] = grads[part, :].reshape((16, 8, PAIR)).astype(jnp.bfloat16)
+        for other_row in others:
+            for a in (1, 2):
+                back_copy(a, other_row, me).start()
+
+    chunk(me // 2, (me + 1 - 2 * (me % 2),))
+
+    def later(step, carry):
+        two = (me // 4 + step // 2) % 2 * 2 + (me // 2 + step) % 2
+        chunk(two, (2 * two, 2 * two + 1))
+        return carry
+
+    lax.fori_loop(1, peers // 2, later, 0)
+    dq = dq_t[...].T * (1.0 / math.sqrt(HD))
+    col_out[0] = dq.reshape((64, 8, PAIR)).astype(jnp.bfloat16)
 
     def give(step, carry):
         target = partner(step)
-        for a in range(3):
-            back_copy(a, target, me).start()
+        back_copy(0, target, me).start()
         return carry
 
     lax.fori_loop(1, peers, give, 0)

time: 34.7 us -> 33.1 us (0.954)
  Pallas kernels: 32 us -> 30.4 us
    pallas_call x1, Pallas kernels: 32 us -> 30.4 us  [local_exchange(): pl.pallas_call(exchange_kernel, out_shape=(pltpu.VMEM((rows, cols // SW,...]
where the time goes in v6:
time: 33.1 us; the launch traced here: 32.9 us
  Pallas kernels  30.4 us (92%)
  other arithmetic  1.93 us (6%)
  between operations  0.64 us (2%)
    pallas_call x1, Pallas kernels, local_exchange(): pl.pallas_call(exchange_kernel, out_shape=(pltpu.VMEM((rows, cols // SW,...  30.4 us
    reshape x2, other arithmetic, local_exchange(): values.astype(jnp.float32).reshape(rows, cols, width)  1.93 us

profile of v6, /device:TPU:0, one launch (start us, length us, event | category | flops | bytes accessed | tf_op | source)
XLA Modules:
  0.0 32.9 jit_solution(8379402817601522556)
XLA Ops:
  0.6 30.4 %shard_map.85 = (bf16[8,2,8,1024]{3,2,1,0:T(8,128)(2,1)S(1)}, bf16[8,2,8,1024]{3,2,1,0:T(8,128)(2,1)S(1)}, bf16[8,2,8,1024]{3,2,1,0:T(8,128)(2,1)S(1)}) custom-call(bf16[8,2,8,1024]{3,2,1,0:T(8,128)(2,1)} %bitcast.15, bf16[8,2,8,1024]{3,2,1,0:T(8,128)(2,1)} %bitcast.16, bf16[8,2,8,1024]{3,2,1,0:T(8,128)(2,1)} %bitcast.17, bf16[8,2,8,1024]{3,2,1,0:T(8,128)(2,1)} %bitcast.18, ...), custom_call_target="tpu_custom_call" | custom-call | tf_op jit(solution)/shard_map/pallas_call | solution.py:470
  31.0 1.1 %bitcast_convert_fusion = (f32[8,16,1024]{2,1,0:T(8,128)}, f32[8,16,1024]{2,1,0:T(8,128)}) fusion(bf16[8,2,8,1024]{3,2,1,0:T(8,128)(2,1)S(1)} %get-tuple-element.8, bf16[8,2,8,1024]{3,2,1,0:T(8,128)(2,1)S(1)} %get-tuple-element.7), kind=kLoop, calls=%fused_computation | loop fusion | flops 262144 | bytes 1572864 | tf_op jit(solution)/shard_map/reshape | solution.py:507
  32.1 0.8 %bitcast_convert_fusion.2 = f32[8,16,1024]{2,1,0:T(8,128)} fusion(bf16[8,2,8,1024]{3,2,1,0:T(8,128)(2,1)S(1)} %get-tuple-element.6), kind=kLoop, calls=%fused_computation.2 | loop fusion | flops 131072 | bytes 786432 | tf_op jit(solution)/shard_map/reshape | solution.py:507

commit v7 on v6

--- a/solution.py
+++ b/solution.py
@@ -348,7 +348,7 @@
     lax.fori_loop(1, peers, send_aux, 0)
 
     def send_keys(step, carry):
-        target = partner(step)
+        target = partner(peers - step)
         for a in (1, 2):
             col_copy(a, target, me).start()
         return carry

time: 33.1 us -> 32.4 us (0.979)
  Pallas kernels: 30.4 us -> 29.7 us
    pallas_call x1, Pallas kernels: 30.4 us -> 29.7 us  [local_exchange(): pl.pallas_call(exchange_kernel, out_shape=(pltpu.VMEM((rows, cols // SW,...]
where the time goes in v7:
time: 32.4 us; the launch traced here: 32.2 us
  Pallas kernels  29.7 us (92%)
  other arithmetic  1.93 us (6%)
  between operations  0.64 us (2%)
    pallas_call x1, Pallas kernels, local_exchange(): pl.pallas_call(exchange_kernel, out_shape=(pltpu.VMEM((rows, cols // SW,...  29.7 us
    reshape x2, other arithmetic, local_exchange(): values.astype(jnp.float32).reshape(rows, cols, width)  1.93 us

profile of v7, /device:TPU:0, one launch (start us, length us, event | category | flops | bytes accessed | tf_op | source)
XLA Modules:
  0.0 32.2 jit_solution(2407504202295396346)
XLA Ops:
  0.6 29.7 %shard_map.85 = (bf16[8,2,8,1024]{3,2,1,0:T(8,128)(2,1)S(1)}, bf16[8,2,8,1024]{3,2,1,0:T(8,128)(2,1)S(1)}, bf16[8,2,8,1024]{3,2,1,0:T(8,128)(2,1)S(1)}) custom-call(bf16[8,2,8,1024]{3,2,1,0:T(8,128)(2,1)} %bitcast.15, bf16[8,2,8,1024]{3,2,1,0:T(8,128)(2,1)} %bitcast.16, bf16[8,2,8,1024]{3,2,1,0:T(8,128)(2,1)} %bitcast.17, bf16[8,2,8,1024]{3,2,1,0:T(8,128)(2,1)} %bitcast.18, ...), custom_call_target="tpu_custom_call" | custom-call | tf_op jit(solution)/shard_map/pallas_call | solution.py:470
  30.3 1.1 %bitcast_convert_fusion = (f32[8,16,1024]{2,1,0:T(8,128)}, f32[8,16,1024]{2,1,0:T(8,128)}) fusion(bf16[8,2,8,1024]{3,2,1,0:T(8,128)(2,1)S(1)} %get-tuple-element.8, bf16[8,2,8,1024]{3,2,1,0:T(8,128)(2,1)S(1)} %get-tuple-element.7), kind=kLoop, calls=%fused_computation | loop fusion | flops 262144 | bytes 1572864 | tf_op jit(solution)/shard_map/reshape | solution.py:507
  31.4 0.8 %bitcast_convert_fusion.2 = f32[8,16,1024]{2,1,0:T(8,128)} fusion(bf16[8,2,8,1024]{3,2,1,0:T(8,128)(2,1)S(1)} %get-tuple-element.6), kind=kLoop, calls=%fused_computation.2 | loop fusion | flops 131072 | bytes 786432 | tf_op jit(solution)/shard_map/reshape | solution.py:507
